TPU v7x, 32 devices: a whole 2x2x4 slice. The times are simulated.
32 devices in a mesh: tok: 8 (over z, x), wid: 4 (over y, core).
Axes of the slice: x: 2, y: 2, z: 4, core: 2. Of those that a mesh axis runs over, the one named last changes fastest.
Arguments:
- acts: bfloat16 [3072, 53248], P('tok', 'wid'), may hold values from -100 to 100
- out_grads: bfloat16 [3072, 16384], P('tok', 'wid'), may hold values from -6 to 6
- test_matrix: bfloat16 [16384, 256], P('wid'), may hold values from -1 to 1
Outputs:
- coeffs: float32 [256, 16384], P('tok', 'wid')
All inputs are finite; a program needn't handle non-finite values.
Results may differ from a plain program's by a relative error of at most 0.01.
Values may be sent and summed in bfloat16 or wider, within the bound.
A program may use at most 64 MiB of HBM per device.

v0:
```python
import math

import jax
import jax.numpy as jnp
from jax import lax
from jax.sharding import PartitionSpec as P


def factor_inverse(gram):
    lower = jnp.linalg.cholesky(gram)
    eye_matrix = jnp.eye(gram.shape[0], dtype=jnp.float32)
    return lax.linalg.triangular_solve(lower, eye_matrix, left_side=True, lower=True)


def shards(acts, out_grads, test_matrix):
    partial_probe = jnp.dot(out_grads, test_matrix, preferred_element_type=jnp.float32)
    probe = lax.psum(partial_probe, "wid").astype(jnp.bfloat16)
    local_sketch = lax.dot_general(
        acts, probe, (((0,), (0,)), ((), ())), preferred_element_type=jnp.float32
    )
    sketch = lax.psum(local_sketch.astype(jnp.bfloat16), "tok").astype(jnp.float32)
    gram_part = jnp.dot(sketch.T, sketch, precision=lax.Precision.HIGHEST)
    gram = lax.psum(gram_part, "wid")
    inverse = factor_inverse(gram)
    basis = jnp.dot(sketch, inverse.T, precision=lax.Precision.HIGHEST).astype(jnp.bfloat16)
    proj_part = jnp.dot(acts, basis, preferred_element_type=jnp.float32)
    proj = lax.psum(proj_part, "wid").astype(jnp.bfloat16)
    scale = 1.0 / math.sqrt(acts.shape[0] * lax.axis_size("tok"))
    term = lax.dot_general(
        proj, out_grads, (((0,), (0,)), ((), ())), preferred_element_type=jnp.float32
    )
    return lax.psum_scatter(term * scale, "tok", scatter_dimension=0, tiled=True)


def solution(mesh):
    return jax.shard_map(
        shards,
        mesh=mesh,
        in_specs=(P("tok", "wid"), P("tok", "wid"), P("wid", None)),
        out_specs=P("tok", "wid"),
        check_vma=False,
    )
```

profile of v0, /device:TPU:0, one launch (start us, length us, event | category | flops | bytes accessed | tf_op | source)
XLA Modules:
  0.0 507.3 jit_solution(18356050534612018119)
XLA Ops:
  6.5 1.9 copy-done
  8.4 3.3 fusion.16
  11.7 17.5 %all-reduce.9 = bf16[384,256]{1,0:T(8,128)(2,1)S(1)} all-reduce(f32[384,256]{1,0:T(8,128)} %fusion.16), channel_id=1, replica_groups=mesh['tok'=8,'wid'=4] {'wid'}, use_global_device_ids=true, to_apply=%region_0.0 | all-reduce | flops 98304 | bytes 589824 | tf_op jit(solution)/shard_map/psum | solution.py:17
  29.2 9.7 %fusion = bf16[13312,256]{0,1:T(8,128)(2,1)} fusion(bf16[384,13312]{1,0:T(8,128)(2,1)} %param.3, bf16[384,256]{1,0:T(8,128)(2,1)S(1)} %all-reduce.9), kind=kOutput, calls=%fused_computation.4 | convolution fusion | flops 2620653568 | bytes 17235968 | tf_op jit(solution)/shard_map/dot_general | solution.py:18
  39.0 226.7 %all-reduce.6.cloned.1.call-done = bf16[13312,256]{0,1:T(8,128)(2,1)} async-done(((bf16[13312,256]{0,1:T(8,128)(2,1)}), bf16[13312,256]{0,1:T(8,128)(2,1)}) %all-reduce.6.cloned.1.call-update) | async-done | bytes 6815760 | tf_op jit(solution)/shard_map/psum | solution.py:21
  265.7 7.5 %fusion.17 = f32[256,256]{0,1:T(8,128)} fusion(bf16[13312,256]{0,1:T(8,128)(2,1)} %all-reduce.6.cloned.1.call-done), kind=kOutput, calls=%fused_computation.41 | convolution fusion | flops 1744830464 | bytes 7077888 | tf_op jit(solution)/shard_map/dot_general | solution.py:22
  273.5 31.2 %all-reduce.8.cloned.1.call-done = f32[256,256]{0,1:T(8,128)} async-done(((f32[256,256]{0,1:T(8,128)}), f32[256,256]{0,1:T(8,128)}) %all-reduce.8.cloned.1.call-update) | async-done | bytes 262160 | tf_op jit(solution)/shard_map/psum | solution.py:23
  304.7 1.1 copy.5
  307.5 11.7 %cholesky.50 = f32[128,128]{1,0:T(8,128)S(1)} custom-call(f32[128,128]{1,0:T(8,128)S(1)} %cholesky.118), custom_call_target="Cholesky" | custom-call | tf_op jit(solution)/shard_map/jit(cholesky)/cholesky | solution.py:10
  319.3 10.4 %custom-call.14 = f32[1,128,128]{1,2,0:T(8,128)} custom-call(f32[1,128,128]{2,1,0:T(8,128)S(1)} %get-tuple-element.26), custom_call_target="InvertDiagBlocksLowerTriangular" | custom-call | tf_op jit(solution)/shard_map/jit(cholesky)/cholesky | solution.py:10
  329.7 1.1 constant_dynamic-update-slice_fusion.1
  330.8 1.7 convolution_subtract_fusion.1
  332.5 12.5 %cholesky.105 = f32[128,128]{1,0:T(8,128)S(1)} custom-call(f32[128,128]{1,0:T(8,128)} %convolution_subtract_fusion.1), custom_call_target="Cholesky" | custom-call | tf_op jit(solution)/shard_map/jit(cholesky)/cholesky | solution.py:10
  348.2 5.5 %while.1 = (s32[]{:T(128)}, f32[256,256]{1,0:T(8,128)S(1)}, s32[2,2]{1,0:T(2,128)S(1)}, f32[2,128,128]{2,1,0:T(8,128)}, s32[]{:T(128)}) while((s32[]{:T(128)}, f32[256,256]{1,0:T(8,128)S(1)}, s32[2,2]{1,0:T(2,128)S(1)}, f32[2,128,128]{2,1,0:T(8,128)}, s32[]{:T(128)}) %tuple.23), condition=%wide.while_cond, body=%wide.while_body.sunk | while | flops 2 | bytes 132205 | solution.py:12
  349.0 2.0 bitcast_dynamic-update-slice_fusion.2
  351.6 2.0 bitcast_dynamic-update-slice_fusion.2
  353.6 21.1 %custom-call.15 = f32[2,128,128]{1,2,0:T(8,128)} custom-call(f32[2,128,128]{2,1,0:T(8,128)} %get-tuple-element.12), custom_call_target="InvertDiagBlocksLowerTriangular" | custom-call | tf_op jit(solution)/shard_map/triangular_solve | solution.py:12
  374.8 1.1 fusion.7
  376.1 1.2 fusion.10
  377.3 9.6 %convolution_convert_fusion = bf16[13312,256]{1,0:T(8,128)(2,1)S(1)} fusion(bf16[13312,256]{0,1:T(8,128)(2,1)} %all-reduce.6.cloned.1.call-done, f32[128,256]{1,0:T(8,128)S(1)} %fusion.10, f32[128,256]{1,0:T(8,128)S(1)} %fusion.7), kind=kOutput, calls=%fused_computation.2 | convolution fusion | flops 10472456192 | bytes 13893632 | tf_op jit(solution)/shard_map/dot_general | solution.py:25
  386.9 7.1 %convolution_bitcast_fusion = f32[384,256]{0,1:T(8,128)} fusion(bf16[13312,256]{1,0:T(8,128)(2,1)S(1)} %convolution_convert_fusion, bf16[384,13312]{1,0:T(8,128)(2,1)} %param.3), kind=kOutput, calls=%fused_computation.6 | convolution fusion | flops 2617245696 | bytes 17432576 | tf_op jit(solution)/shard_map/dot_general | solution.py:26
  394.0 15.1 %all-reduce.10 = bf16[384,256]{0,1:T(8,128)(2,1)S(1)} all-reduce(f32[384,256]{0,1:T(8,128)} %convolution_bitcast_fusion), channel_id=1, replica_groups=mesh['tok'=8,'wid'=4] {'wid'}, use_global_device_ids=true, to_apply=%region_7.8 | all-reduce | flops 98304 | bytes 589824 | tf_op jit(solution)/shard_map/psum | solution.py:27
  409.1 3.2 convolution_multiply_fusion
  412.3 88.4 %reduce-scatter.2.cloned.1.call-done = f32[32,4096]{1,0:T(8,128)} async-done(((f32[256,4096]{1,0:T(8,128)}), f32[32,4096]{1,0:T(8,128)}) %reduce-scatter.2.cloned.1.call-update) | async-done | bytes 524304 | tf_op jit(solution)/shard_map/reduce_scatter | solution.py:32
  (27 shorter events, 5.4 us)
Async XLA Ops:
  6.5 1.9 copy-start
  6.5 259.2 %all-reduce.6.cloned.1.call-start = ((), (), s32[]{:S(2)}) async-start(), calls=%async_computation.1 | async-start | bytes 13631488 | tf_op jit(solution)/shard_map/psum | solution.py:21
  39.0 265.7 %all-reduce.8.cloned.1.call-start = ((), (), s32[]{:S(2)}) async-start(), calls=%async_computation.2 | async-start | bytes 524288 | tf_op jit(solution)/shard_map/psum | solution.py:23
  273.3 227.5 %reduce-scatter.2.cloned.1.call-start = ((), (), s32[]{:S(2)}) async-start(), calls=%async_computation.3 | async-start | bytes 4718592 | tf_op jit(solution)/shard_map/reduce_scatter | solution.py:32
  306.8 0.7 copy-start.2
  345.1 2.0 copy-start.1
Sparse Core Ops, SparseCore 0:
  39.1 226.5 all-reduce.5
  273.4 31.3 all-reduce.7
  412.5 88.2 reduce-scatter.1
where the time goes:
time: 508 us; the launch traced here: 507 us
  waiting for transfers between devices  346 us (68%)
  other arithmetic  58.6 us (12%)
  matrix products  45.8 us (9%)
  blocking collectives  32.6 us (6%)
  between operations  14.5 us (3%)
  local copies, waits for them, and re-layouts  9.05 us (2%)
    psum x1, waiting for transfers between devices, shards(): lax.psum(local_sketch.astype(jnp.bfloat16), 'tok').astype(jnp.float32)  227 us
    reduce_scatter x1, waiting for transfers between devices, shards(): lax.psum_scatter(term * scale, 'tok', scatter_dimension=0, tiled=True)  88.4 us
    another operation x6, other arithmetic, factor_inverse(): lower = jnp.linalg.cholesky(gram)  35.5 us
    psum x1, waiting for transfers between devices, shards(): gram = lax.psum(gram_part, 'wid')  31.2 us
    another operation x3, other arithmetic, factor_inverse(): lax.linalg.triangular_solve(lower, eye_matrix, left_side=True, lower=True)  22.1 us
    psum x1, blocking collectives, shards(): probe = lax.psum(partial_probe, 'wid').astype(jnp.bfloat16)  17.5 us
    psum x1, blocking collectives, shards(): proj = lax.psum(proj_part, 'wid').astype(jnp.bfloat16)  15.1 us
  transfers between devices with their start and end apart: 3, of which 3 were waited for; matrix products, arithmetic and copies ran while one was open for 0% of the time, Pallas kernels for 0%

commit v1 on v0

v1 whole, which is shorter than its diff:
```python
import functools
import math

import jax
import jax.numpy as jnp
from jax import lax
from jax.experimental import pallas as pl
from jax.experimental.pallas import tpu as pltpu
from jax.sharding import PartitionSpec as P

MESH = pl.DeviceIdType.MESH
F32 = jnp.float32
BF16 = jnp.bfloat16
VMEM_LIMIT = 60 * 1024 * 1024
WAYS = (0, 1)
PIECES = 2


def nt(a, b, precision=None):
    return lax.dot_general(
        a, b, (((1,), (1,)), ((), ())), preferred_element_type=F32, precision=precision
    )


class Ring:
    def __init__(self, n):
        self.n, self.rows, self.cols = n, 4, n // 4
        self.body = self.rows * (self.cols - 1)
        self.tok = lax.axis_index("tok")
        self.pos = self.pos_of(self.tok)

    def pos_of(self, tok):
        r, c = lax.div(tok, self.cols), lax.rem(tok, self.cols)
        odd = lax.rem(r, 2)
        inner = lax.div(c + self.cols - 1, self.cols)
        along = r * (self.cols - 1) + (1 - odd) * (c - 1) + odd * (self.cols - 1 - c)
        back = self.body + self.rows - 1 - r
        return inner * along + (1 - inner) * back

    def tok_of(self, pos):
        last = lax.div(pos, self.body)
        r, k = lax.div(pos, self.cols - 1), lax.rem(pos, self.cols - 1)
        odd = lax.rem(r, 2)
        along = r * self.cols + (1 - odd) * (k + 1) + odd * (self.cols - 1 - k)
        back = (self.rows - 1 - (pos - self.body)) * self.cols
        return (1 - last) * along + last * back

    def at(self, offset):
        return lax.rem(self.pos + offset + 2 * self.n, self.n)

    def neighbours(self):
        return self.tok_of(self.at(1)), self.tok_of(self.at(-1))

    def barrier(self):
        sem = pltpu.get_barrier_semaphore()
        for other in self.neighbours():
            pl.semaphore_signal(
                sem, inc=1, device_id={"tok": other}, device_id_type=MESH
            )
        pl.semaphore_wait(sem, 2)


def ring_scatter(ring, term, store, send, recv, send_sems, recv_sems):
    n = ring.n
    dest = ring.neighbours()

    def copy(way, step, piece):
        return pltpu.make_async_remote_copy(
            src_ref=send.at[way, step, piece],
            dst_ref=recv.at[way, step, piece],
            send_sem=send_sems.at[way, step, piece],
            recv_sem=recv_sems.at[way, step, piece],
            device_id={"tok": dest[way]},
            device_id_type=MESH,
        )

    def block(way, step):
        return ring.at(-1 - step) if way == 0 else ring.at(1 + step)

    for piece in range(PIECES):
        for way in WAYS:
            send[way, 0, piece] = term(way, piece, block(way, 0)).astype(BF16)
            copy(way, 0, piece).start()

    def step(s, carry):
        for piece in range(PIECES):
            for way in WAYS:
                own = term(way, piece, block(way, s))
                copy(way, s - 1, piece).wait_recv()
                total = own + recv[way, s - 1, piece].astype(F32)
                send[way, s, piece] = total.astype(BF16)
                copy(way, s, piece).start()
        return carry

    lax.fori_loop(1, n - 1, step, 0)
    for piece in range(PIECES):
        for way in WAYS:
            own = term(way, piece, ring.pos)
            copy(way, n - 2, piece).wait_recv()
            store(way, piece, own + recv[way, n - 2, piece].astype(F32))

    def drain(s, carry):
        for piece in range(PIECES):
            for way in WAYS:
                copy(way, s, piece).wait_send()
        return carry

    lax.fori_loop(0, n - 1, drain, 0)


def sketch_kernel(n, acts, probe_t, out, send, recv, send_sems, recv_sems):
    ring = Ring(n)
    width = out.shape[1]
    rows = out.shape[0] // (2 * PIECES)

    def term(way, piece, pos):
        first = (way * PIECES + piece) * rows
        columns = pl.ds(pl.multiple_of(pos * width, 128), width)
        return jnp.dot(
            probe_t[first : first + rows, :], acts[:, columns], preferred_element_type=F32
        )

    def store(way, piece, total):
        first = (way * PIECES + piece) * rows
        out[first : first + rows, :] = total.astype(BF16)

    ring.barrier()
    ring_scatter(ring, term, store, send, recv, send_sems, recv_sems)


def gather_kernel(n, acts, own, mixed, gram, held, send_sems, recv_sems):
    ring = Ring(n)
    width = own.shape[1]
    rows = own.shape[0] // (2 * PIECES)
    half = own.shape[0] // 2
    dest = ring.neighbours()

    def copy(way, step, piece, first=False):
        pos = ring.at(-step) if way == 0 else ring.at(step)
        lines = pl.ds((way * PIECES + piece) * rows, rows)
        return pltpu.make_async_remote_copy(
            src_ref=own.at[lines] if first else held.at[pos, lines],
            dst_ref=held.at[pos, lines],
            send_sem=send_sems.at[way, step, piece],
            recv_sem=recv_sems.at[way, step, piece],
            device_id={"tok": dest[way]},
            device_id_type=MESH,
        )

    def add(way, pos, ref):
        columns = pl.ds(pl.multiple_of(pos * width, 128), width)
        lanes = slice(way * half, (way + 1) * half)
        mixed[:, lanes] += nt(acts[:, columns], ref[lanes, :])

    ring.barrier()
    for piece in range(PIECES):
        for way in WAYS:
            copy(way, 0, piece, True).start()
    mixed[...] = jnp.zeros_like(mixed)
    gram[...] = nt(own[...], own[...])
    for way in WAYS:
        add(way, ring.pos, own)

    def step(s, carry):
        for piece in range(PIECES):
            for way in WAYS:
                copy(way, s - 1, piece).wait_recv()
                copy(way, s, piece).start()
        for way in WAYS:
            pos = ring.at(-s) if way == 0 else ring.at(s)
            add(way, pos, held.at[pos])
        return carry

    lax.fori_loop(1, n - 1, step, 0)
    for piece in range(PIECES):
        for way in WAYS:
            copy(way, n - 2, piece).wait_recv()
    for way in WAYS:
        pos = ring.at(1 - n) if way == 0 else ring.at(n - 1)
        add(way, pos, held.at[pos])

    def more(s, carry):
        block = held.at[ring.at(s)]
        gram[...] += nt(block[...], block[...])
        return carry

    lax.fori_loop(1, n, more, 0)

    def drain(s, carry):
        for piece in range(PIECES):
            for way in WAYS:
                copy(way, s, piece, False).wait_send()
        return carry

    lax.fori_loop(0, n - 1, drain, 0)


def coeffs_kernel(n, scale, mixed, inverse, grads, out, terms, send, recv, send_sems, recv_sems):
    ring = Ring(n)
    rows, width = out.shape
    part = width // (2 * PIECES)

    def term(way, piece, pos):
        first = (way * PIECES + piece) * part
        return terms[ring.tok_of(pos), :, first : first + part]

    def store(way, piece, total):
        first = (way * PIECES + piece) * part
        out[:, first : first + part] = total

    ring.barrier()
    proj_t = nt(inverse[...], mixed[...], lax.Precision.HIGHEST).astype(BF16)
    for first in range(0, width, 512 if width % 512 == 0 else width):
        last = min(width, first + 512) if width % 512 == 0 else width
        piece = jnp.dot(proj_t, grads[:, first:last], preferred_element_type=F32)
        terms[:, :, first:last] = (piece * scale).reshape(n, rows, last - first)
    ring_scatter(ring, term, store, send, recv, send_sems, recv_sems)


def call(kernel, outs, scratch, number, *args):
    vmem = pl.BlockSpec(memory_space=pltpu.VMEM)
    return pl.pallas_call(
        kernel,
        out_shape=outs,
        in_specs=[vmem] * len(args),
        out_specs=jax.tree.map(lambda _: vmem, outs),
        scratch_shapes=scratch,
        compiler_params=pltpu.CompilerParams(
            collective_id=number, has_side_effects=True, vmem_limit_bytes=VMEM_LIMIT
        ),
    )(*args)


def sems(n):
    return [pltpu.SemaphoreType.DMA((2, n - 1, PIECES)) for _ in range(2)]


def slots(n, rows, width):
    return [pltpu.VMEM((2, n - 1, PIECES, rows, width), BF16) for _ in range(2)]


def factor_inverse(gram):
    lower = jnp.linalg.cholesky(gram)
    eye_matrix = jnp.eye(gram.shape[0], dtype=F32)
    return lax.linalg.triangular_solve(lower, eye_matrix, left_side=True, lower=True)


def ring_shards(n, acts, out_grads, test_matrix):
    partial_probe = jnp.dot(out_grads, test_matrix, preferred_element_type=F32)
    probe = lax.psum(partial_probe, "wid").astype(BF16)
    tokens, hidden = acts.shape
    rank, model = test_matrix.shape[1], out_grads.shape[1]
    width = hidden // n
    struct = jax.ShapeDtypeStruct
    rows_t = call(
        functools.partial(sketch_kernel, n),
        struct((rank, width), BF16),
        slots(n, rank // (2 * PIECES), width) + sems(n),
        0, acts, probe.T,
    )
    mixed_part, gram_part = call(
        functools.partial(gather_kernel, n),
        [struct((tokens, rank), F32), struct((rank, rank), F32)],
        [pltpu.VMEM((n, rank, width), BF16)] + sems(n),
        1, acts, rows_t,
    )
    both = lax.psum(jnp.concatenate([mixed_part, gram_part]), "wid")
    mixed, gram = both[:tokens], both[tokens:]
    inverse = factor_inverse(gram)
    scale = 1.0 / math.sqrt(tokens * n)
    rows = rank // n
    return call(
        functools.partial(coeffs_kernel, n, scale),
        struct((rows, model), F32),
        [pltpu.VMEM((n, rows, model), F32)]
        + slots(n, rows, model // (2 * PIECES)) + sems(n),
        2, mixed, inverse, out_grads,
    )


def plain_shards(acts, out_grads, test_matrix):
    partial_probe = jnp.dot(out_grads, test_matrix, preferred_element_type=F32)
    probe = lax.psum(partial_probe, "wid").astype(BF16)
    local_sketch = lax.dot_general(
        acts, probe, (((0,), (0,)), ((), ())), preferred_element_type=F32
    )
    sketch = lax.psum(local_sketch.astype(BF16), "tok")
    gram = lax.psum(
        lax.dot_general(sketch, sketch, (((0,), (0,)), ((), ())), preferred_element_type=F32),
        "wid",
    )
    inverse = factor_inverse(gram)
    mixed = lax.psum(jnp.dot(acts, sketch, preferred_element_type=F32), "wid")
    proj = jnp.dot(mixed, inverse.T, precision=lax.Precision.HIGHEST).astype(BF16)
    scale = 1.0 / math.sqrt(acts.shape[0] * lax.axis_size("tok"))
    term = lax.dot_general(
        proj, out_grads, (((0,), (0,)), ((), ())), preferred_element_type=F32
    )
    return lax.psum_scatter(term * scale, "tok", scatter_dimension=0, tiled=True)


def solution(mesh):
    n = mesh.shape["tok"]

    def shards(acts, out_grads, test_matrix):
        width, left = divmod(acts.shape[1], n)
        if n % 4 == 0 and n > 4 and left == 0 and width % 128 == 0:
            return ring_shards(n, acts, out_grads, test_matrix)
        return plain_shards(acts, out_grads, test_matrix)

    return jax.shard_map(
        shards,
        mesh=mesh,
        in_specs=(P("tok", "wid"), P("tok", "wid"), P("wid", None)),
        out_specs=P("tok", "wid"),
        check_vma=False,
    )
```

time: 508 us -> 324 us (0.64)
  waiting for transfers between devices: 346 us -> 35.1 us
  Pallas kernels: 0 us -> 183 us
  matrix products: 45.8 us -> 4.49 us
  blocking collectives: 32.6 us -> 17.4 us
    psum x2 -> x1, waiting for transfers between devices: 258 us -> 35.1 us  [ring_shards(): both = lax.psum(jnp.concatenate([mixed_part, gram_part]), 'wid')]
    pallas_call x0 -> x3, Pallas kernels: none -> 183 us  [call(): pl.pallas_call(kernel, out_shape=outs, in_specs=[vmem] * len(args), out_s...]
    reduce_scatter x1 -> x0, waiting for transfers between devices: 88.4 us -> none  [shards(): lax.psum_scatter(term * scale, 'tok', scatter_dimension=0, tiled=True)]
    dot_general x6 -> x1, matrix products: 40.5 us -> 3.18 us  [ring_shards(): partial_probe = jnp.dot(out_grads, test_matrix, preferred_element_type=F32)]
    psum x2 -> x1, blocking collectives: 32.6 us -> 17.4 us  [ring_shards(): probe = lax.psum(partial_probe, 'wid').astype(BF16)]
    another operation x3 -> x4, other arithmetic: 22.1 us -> 21.2 us  [factor_inverse(): lax.linalg.triangular_solve(lower, eye_matrix, left_side=True, lower=True)]
  transfers between devices with their start and end apart: 3 -> 1, of which waited for: 3 -> 1; matrix products, arithmetic and copies ran while one was open for 0% -> 0% of each run, Pallas kernels for 0% -> 0%
where the time goes in v1:
time: 324 us
  Pallas kernels  183 us (56%)
  other arithmetic  58.2 us (18%)
  waiting for transfers between devices  35.1 us (11%)
  blocking collectives  17.4 us (5%)
  between operations  14.8 us (5%)
  local copies, waits for them, and re-layouts  10.7 us (3%)
  matrix products  4.49 us (1%)
    pallas_call x3, Pallas kernels, call(): pl.pallas_call(kernel, out_shape=outs, in_specs=[vmem] * len(args), out_s...  183 us
    psum x1, waiting for transfers between devices, ring_shards(): both = lax.psum(jnp.concatenate([mixed_part, gram_part]), 'wid')  35.1 us
    another operation x6, other arithmetic, factor_inverse(): lower = jnp.linalg.cholesky(gram)  34 us
    another operation x4, other arithmetic, factor_inverse(): lax.linalg.triangular_solve(lower, eye_matrix, left_side=True, lower=True)  21.2 us
    psum x1, blocking collectives, ring_shards(): probe = lax.psum(partial_probe, 'wid').astype(BF16)  17.4 us
  transfers between devices with their start and end apart: 1, of which 1 were waited for; matrix products, arithmetic and copies ran while one was open for 0% of the time, Pallas kernels for 0%

profile of v1, /device:TPU:0, one launch (start us, length us, event | category | flops | bytes accessed | tf_op | source)
XLA Modules:
  0.0 323.9 jit_solution(1144188839740288397)
XLA Ops:
  6.5 1.6 copy-done
  8.1 3.2 fusion.9
  11.3 17.4 %all-reduce.5 = bf16[384,256]{0,1:T(8,128)(2,1)} all-reduce(f32[384,256]{0,1:T(8,128)S(1)} %fusion.9), channel_id=1, replica_groups=mesh['tok'=8,'wid'=4] {'wid'}, use_global_device_ids=true, to_apply=%region_0.0 | all-reduce | flops 98304 | bytes 589824 | tf_op jit(solution)/shard_map/psum | solution.py:250
  28.7 73.1 %shard_map.37.own = bf16[256,1664]{1,0:T(8,128)(2,1)} custom-call(bf16[384,13312]{1,0:T(8,128)(2,1)} %acts.3, bf16[256,384]{1,0:T(8,128)(2,1)} %bitcast.36), custom_call_target="tpu_custom_call" | custom-call | tf_op jit(solution)/shard_map/pallas_call | solution.py:222
  101.8 75.0 %shard_map.38 = (f32[384,256]{1,0:T(8,128)}, f32[256,256]{1,0:T(8,128)}) custom-call(bf16[384,13312]{1,0:T(8,128)(2,1)} %acts.3, bf16[256,1664]{1,0:T(8,128)(2,1)} %shard_map.37.own), custom_call_target="tpu_custom_call" | custom-call | tf_op jit(solution)/shard_map/pallas_call | solution.py:222
  176.7 2.0 pad_maximum_fusion
  178.8 35.1 %all-reduce.4.cloned.1.call-done = f32[640,256]{1,0:T(8,128)} async-done(((f32[640,256]{1,0:T(8,128)}), f32[640,256]{1,0:T(8,128)}) %all-reduce.4.cloned.1.call-update) | async-done | bytes 655376 | tf_op jit(solution)/shard_map/psum | solution.py:267
  213.9 1.0 slice.63
  215.0 1.0 fusion
  216.0 11.7 %cholesky.50 = f32[128,128]{1,0:T(8,128)S(1)} custom-call(f32[128,128]{1,0:T(8,128)S(1)} %cholesky.118), custom_call_target="Cholesky" | custom-call | tf_op jit(solution)/shard_map/jit(cholesky)/cholesky | solution.py:243
  227.8 9.8 %custom-call.14 = f32[1,128,128]{1,2,0:T(8,128)S(1)} custom-call(f32[1,128,128]{2,1,0:T(8,128)S(1)} %get-tuple-element.30), custom_call_target="InvertDiagBlocksLowerTriangular" | custom-call | tf_op jit(solution)/shard_map/jit(cholesky)/cholesky | solution.py:243
  238.1 11.7 %cholesky.105 = f32[128,128]{1,0:T(8,128)S(1)} custom-call(f32[128,128]{1,0:T(8,128)S(1)} %convolution_subtract_fusion.1), custom_call_target="Cholesky" | custom-call | tf_op jit(solution)/shard_map/jit(cholesky)/cholesky | solution.py:243
  249.9 0.7 compare_reduce_fusion
  251.9 5.3 %while.1 = (s32[]{:T(128)}, f32[256,256]{1,0:T(8,128)S(1)}, s32[2,2]{1,0:T(2,128)S(1)}, f32[2,128,128]{2,1,0:T(8,128)}, s32[]{:T(128)}) while((s32[]{:T(128)}, f32[256,256]{1,0:T(8,128)S(1)}, s32[2,2]{1,0:T(2,128)S(1)}, f32[2,128,128]{2,1,0:T(8,128)}, s32[]{:T(128)}) %tuple.23), condition=%wide.while_cond, body=%wide.while_body.sunk | while | flops 2 | bytes 132705 | solution.py:245
  251.9 0.6 fusion.17
  252.6 2.0 bitcast_dynamic-update-slice_fusion.2
  254.6 0.6 fusion.17
  255.2 2.0 bitcast_dynamic-update-slice_fusion.2
  257.2 20.5 %custom-call.15 = f32[2,128,128]{1,2,0:T(8,128)S(1)} custom-call(f32[2,128,128]{2,1,0:T(8,128)} %get-tuple-element.16), custom_call_target="InvertDiagBlocksLowerTriangular" | custom-call | tf_op jit(solution)/shard_map/triangular_solve | solution.py:245
  278.2 0.3 fusion.4
  278.5 0.7 pad_maximum_fusion.1.inverse
  279.3 0.8 slice.62.mixed
  280.0 35.2 %shard_map.39 = f32[32,4096]{1,0:T(8,128)} custom-call(f32[384,256]{1,0:T(8,128)} %slice.62.mixed, f32[256,256]{1,0:T(8,128)} %pad_maximum_fusion.1.inverse, bf16[384,4096]{1,0:T(8,128)(2,1)} %grads.1), custom_call_target="tpu_custom_call" | custom-call | tf_op jit(solution)/shard_map/pallas_call | solution.py:222
  315.2 1.9 copy.23
  (21 shorter events, 1.4 us)
Async XLA Ops:
  6.5 1.6 copy-start
  6.5 207.3 %all-reduce.4.cloned.1.call-start = ((), (), s32[]{:S(2)}) async-start(), calls=%async_computation | async-start | bytes 1310720 | tf_op jit(solution)/shard_map/psum | solution.py:267
  213.9 65.4 %copy-start.1 = (f32[640,256]{1,0:T(8,128)S(1)}, f32[640,256]{1,0:T(8,128)}, u32[]{:S(2)}) copy-start(f32[640,256]{1,0:T(8,128)} %all-reduce.4.cloned.1.call-done) | copy-start | bytes 1966084
Sparse Core Ops, SparseCore 0:
  178.9 34.9 all-reduce.3

commit v2 on v1

--- a/solution.py
+++ b/solution.py
@@ -51,13 +51,52 @@
     def neighbours(self):
         return self.tok_of(self.at(1)), self.tok_of(self.at(-1))
 
-    def barrier(self):
+    def barrier(self, peers=1):
         sem = pltpu.get_barrier_semaphore()
+        me = lax.axis_index("wid")
+        for k in range(1, peers):
+            other = lax.rem(me + k, peers)
+            pl.semaphore_signal(
+                sem, inc=1, device_id={"wid": other}, device_id_type=MESH
+            )
         for other in self.neighbours():
             pl.semaphore_signal(
                 sem, inc=1, device_id={"tok": other}, device_id_type=MESH
             )
-        pl.semaphore_wait(sem, 2)
+        pl.semaphore_wait(sem, 1 + peers)
+
+
+def wid_sum(m, part, got, mine, out, sems):
+    me = lax.axis_index("wid")
+    share = part.shape[0] // m
+
+    def lines(index):
+        return pl.ds(pl.multiple_of(index * share, 16), share)
+
+    def copy(phase, k):
+        other = lax.rem(me + k, m)
+        return pltpu.make_async_remote_copy(
+            src_ref=mine if phase else part.at[lines(other)],
+            dst_ref=out.at[lines(me)] if phase else got.at[k - 1],
+            send_sem=sems.at[phase, 0, k - 1],
+            recv_sem=sems.at[phase, 1, k - 1],
+            device_id={"wid": other},
+            device_id_type=MESH,
+        )
+
+    for k in range(1, m):
+        copy(0, k).start()
+    total = part[lines(me), :]
+    for k in range(1, m):
+        copy(0, k).wait_recv()
+        total = total + got[k - 1]
+    mine[...] = total.astype(mine.dtype)
+    for k in range(1, m):
+        copy(1, k).start()
+    out[lines(me), :] = total.astype(out.dtype)
+    for k in range(1, m):
+        copy(0, k).wait_send()
+        copy(1, k).wait()
 
 
 def ring_scatter(ring, term, store, send, recv, send_sems, recv_sems):
@@ -108,7 +147,10 @@
     lax.fori_loop(0, n - 1, drain, 0)
 
 
-def sketch_kernel(n, acts, probe_t, out, send, recv, send_sems, recv_sems):
+def sketch_kernel(
+    n, m, acts, grads, test, out, part, got, mine, probe_t, wid_sems,
+    send, recv, send_sems, recv_sems,
+):
     ring = Ring(n)
     width = out.shape[1]
     rows = out.shape[0] // (2 * PIECES)
@@ -124,11 +166,18 @@
         first = (way * PIECES + piece) * rows
         out[first : first + rows, :] = total.astype(BF16)
 
-    ring.barrier()
+    ring.barrier(m)
+    part[...] = jnp.dot(grads[...], test[...], preferred_element_type=F32).T
+    wid_sum(m, part, got, mine, probe_t, wid_sems)
     ring_scatter(ring, term, store, send, recv, send_sems, recv_sems)
 
 
-def gather_kernel(n, acts, own, mixed, gram, held, send_sems, recv_sems):
+def gather_kernel(
+    n, m, acts, own, out_mixed, out_gram, part, got, mine, full, wid_sems,
+    held, send_sems, recv_sems,
+):
+    tokens = acts.shape[0]
+    mixed, gram = part.at[0:tokens], part.at[tokens : part.shape[0]]
     ring = Ring(n)
     width = own.shape[1]
     rows = own.shape[0] // (2 * PIECES)
@@ -152,7 +201,7 @@
         lanes = slice(way * half, (way + 1) * half)
         mixed[:, lanes] += nt(acts[:, columns], ref[lanes, :])
 
-    ring.barrier()
+    ring.barrier(m)
     for piece in range(PIECES):
         for way in WAYS:
             copy(way, 0, piece, True).start()
@@ -185,6 +234,9 @@
         return carry
 
     lax.fori_loop(1, n, more, 0)
+    wid_sum(m, part, got, mine, full, wid_sems)
+    out_mixed[...] = full[0:tokens, :]
+    out_gram[...] = full[tokens : part.shape[0], :]
 
     def drain(s, carry):
         for piece in range(PIECES):
@@ -195,7 +247,28 @@
     lax.fori_loop(0, n - 1, drain, 0)
 
 
-def coeffs_kernel(n, scale, mixed, inverse, grads, out, terms, send, recv, send_sems, recv_sems):
+def invert(lower, inverse):
+    i = lax.broadcasted_iota(jnp.int32, lower.shape, 0)
+    j = lax.broadcasted_iota(jnp.int32, lower.shape, 1)
+    inverse[...] = jnp.where(i == j, 1.0 / jnp.where(i == j, lower[...], 1.0), 0.0)
+
+    def level(k, carry):
+        i_block, j_block = lax.shift_right_logical(i, k), lax.shift_right_logical(j, k)
+        same = lax.shift_right_logical(i, k + 1) == lax.shift_right_logical(j, k + 1)
+        below = jnp.where(jnp.logical_and(same, i_block > j_block), lower[...], 0.0)
+        high = lax.Precision.HIGHEST
+        right = jnp.dot(below, inverse[...], precision=high, preferred_element_type=F32)
+        inverse[...] -= jnp.dot(
+            inverse[...], right, precision=high, preferred_element_type=F32
+        )
+        return carry
+
+    lax.fori_loop(0, (lower.shape[0] - 1).bit_length(), level, 0)
+
+
+def coeffs_kernel(
+    n, scale, mixed, lower, grads, out, inverse, terms, send, recv, send_sems, recv_sems
+):
     ring = Ring(n)
     rows, width = out.shape
     part = width // (2 * PIECES)
@@ -209,6 +282,7 @@
         out[:, first : first + part] = total
 
     ring.barrier()
+    invert(lower, inverse)
     proj_t = nt(inverse[...], mixed[...], lax.Precision.HIGHEST).astype(BF16)
     for first in range(0, width, 512 if width % 512 == 0 else width):
         last = min(width, first + 512) if width % 512 == 0 else width
@@ -245,36 +319,44 @@
     return lax.linalg.triangular_solve(lower, eye_matrix, left_side=True, lower=True)
 
 
-def ring_shards(n, acts, out_grads, test_matrix):
-    partial_probe = jnp.dot(out_grads, test_matrix, preferred_element_type=F32)
-    probe = lax.psum(partial_probe, "wid").astype(BF16)
+def wid_scratch(m, rows, width, dtype):
+    return [
+        pltpu.VMEM((rows, width), F32),
+        pltpu.VMEM((m - 1, rows // m, width), F32),
+        pltpu.VMEM((rows // m, width), dtype),
+        pltpu.VMEM((rows, width), dtype),
+        pltpu.SemaphoreType.DMA((2, 2, m - 1)),
+    ]
+
+
+def ring_shards(n, m, acts, out_grads, test_matrix):
     tokens, hidden = acts.shape
     rank, model = test_matrix.shape[1], out_grads.shape[1]
     width = hidden // n
     struct = jax.ShapeDtypeStruct
     rows_t = call(
-        functools.partial(sketch_kernel, n),
+        functools.partial(sketch_kernel, n, m),
         struct((rank, width), BF16),
-        slots(n, rank // (2 * PIECES), width) + sems(n),
-        0, acts, probe.T,
-    )
-    mixed_part, gram_part = call(
-        functools.partial(gather_kernel, n),
+        wid_scratch(m, rank, tokens, BF16)
+        + slots(n, rank // (2 * PIECES), width) + sems(n),
+        0, acts, out_grads, test_matrix,
+    )
+    mixed, gram = call(
+        functools.partial(gather_kernel, n, m),
         [struct((tokens, rank), F32), struct((rank, rank), F32)],
-        [pltpu.VMEM((n, rank, width), BF16)] + sems(n),
+        wid_scratch(m, tokens + rank, rank, F32)
+        + [pltpu.VMEM((n, rank, width), BF16)] + sems(n),
         1, acts, rows_t,
     )
-    both = lax.psum(jnp.concatenate([mixed_part, gram_part]), "wid")
-    mixed, gram = both[:tokens], both[tokens:]
-    inverse = factor_inverse(gram)
+    lower = jnp.linalg.cholesky(gram)
     scale = 1.0 / math.sqrt(tokens * n)
     rows = rank // n
     return call(
         functools.partial(coeffs_kernel, n, scale),
         struct((rows, model), F32),
-        [pltpu.VMEM((n, rows, model), F32)]
+        [pltpu.VMEM((rank, rank), F32), pltpu.VMEM((n, rows, model), F32)]
         + slots(n, rows, model // (2 * PIECES)) + sems(n),
-        2, mixed, inverse, out_grads,
+        2, mixed, lower, out_grads,
     )
 
 
@@ -300,12 +382,13 @@
 
 
 def solution(mesh):
-    n = mesh.shape["tok"]
+    n, m = mesh.shape["tok"], mesh.shape["wid"]
 
     def shards(acts, out_grads, test_matrix):
         width, left = divmod(acts.shape[1], n)
-        if n % 4 == 0 and n > 4 and left == 0 and width % 128 == 0:
-            return ring_shards(n, acts, out_grads, test_matrix)
+        even = acts.shape[0] % (16 * m) == 0 and test_matrix.shape[1] % (16 * m) == 0
+        if n % 4 == 0 and n > 4 and m > 1 and even and left == 0 and width % 128 == 0:
+            return ring_shards(n, m, acts, out_grads, test_matrix)
         return plain_shards(acts, out_grads, test_matrix)
 
     return jax.shard_map(

time: 324 us -> 263 us (0.81)
  Pallas kernels: 183 us -> 222 us
  waiting for transfers between devices: 35.1 us -> 0 us
  other arithmetic: 58.2 us -> 35.7 us
  blocking collectives: 17.4 us -> 0 us
  between operations: 14.8 us -> 1.41 us
  local copies, waits for them, and re-layouts: 10.7 us -> 2.97 us
  matrix products: 4.49 us -> 0.47 us
    pallas_call x3, Pallas kernels: 183 us -> 222 us  [call(): pl.pallas_call(kernel, out_shape=outs, in_specs=[vmem] * len(args), out_s...]
    psum x1 -> x0, waiting for transfers between devices: 35.1 us -> none  [ring_shards(): both = lax.psum(jnp.concatenate([mixed_part, gram_part]), 'wid')]
    another operation x10 -> x6, other arithmetic: 55.2 us -> 34 us  [ring_shards(): lower = jnp.linalg.cholesky(gram)]
    psum x1 -> x0, blocking collectives: 17.4 us -> none  [ring_shards(): probe = lax.psum(partial_probe, 'wid').astype(BF16)]
    another operation x9 -> x2, local copies, waits for them, and re-layouts: 5.34 us -> 0.03 us  [ring_shards(): lower = jnp.linalg.cholesky(gram)]
  transfers between devices with their start and end apart: 1 -> 0, of which waited for: 1 -> 0; matrix products, arithmetic and copies ran while one was open for 0% -> 0% of each run, Pallas kernels for 0% -> 0%
where the time goes in v2:
time: 263 us
  Pallas kernels  222 us (84%)
  other arithmetic  35.7 us (14%)
  local copies, waits for them, and re-layouts  2.97 us (1%)
    pallas_call x3, Pallas kernels, call(): pl.pallas_call(kernel, out_shape=outs, in_specs=[vmem] * len(args), out_s...  222 us
    another operation x6, other arithmetic, ring_shards(): lower = jnp.linalg.cholesky(gram)  34 us

profile of v2, /device:TPU:0, one launch (start us, length us, event | category | flops | bytes accessed | tf_op | source)
XLA Modules:
  0.0 262.5 jit_solution(8672369913155111460)
XLA Ops:
  0.0 88.5 %shard_map.37.own = bf16[256,1664]{1,0:T(8,128)(2,1)} custom-call(bf16[384,13312]{1,0:T(8,128)(2,1)} %acts.3, bf16[384,4096]{1,0:T(8,128)(2,1)} %grads.3, bf16[4096,256]{1,0:T(8,128)(2,1)} %test.1), custom_call_target="tpu_custom_call" | custom-call | tf_op jit(solution)/shard_map/pallas_call | solution.py:296
  88.5 91.1 %shard_map.38 = (f32[384,256]{1,0:T(8,128)}, f32[256,256]{1,0:T(8,128)}) custom-call(bf16[384,13312]{1,0:T(8,128)(2,1)} %acts.3, bf16[256,1664]{1,0:T(8,128)(2,1)} %shard_map.37.own), custom_call_target="tpu_custom_call" | custom-call | tf_op jit(solution)/shard_map/pallas_call | solution.py:296
  179.7 1.1 copy.4
  180.8 1.0 fusion
  181.8 11.7 %cholesky.50 = f32[128,128]{1,0:T(8,128)S(1)} custom-call(f32[128,128]{1,0:T(8,128)S(1)} %cholesky.118), custom_call_target="Cholesky" | custom-call | tf_op jit(solution)/shard_map/jit(cholesky)/cholesky | solution.py:351
  193.5 9.8 %custom-call.11 = f32[1,128,128]{1,2,0:T(8,128)S(1)} custom-call(f32[1,128,128]{2,1,0:T(8,128)S(1)} %get-tuple-element.12), custom_call_target="InvertDiagBlocksLowerTriangular" | custom-call | tf_op jit(solution)/shard_map/jit(cholesky)/cholesky | solution.py:351
  203.4 0.2 constant_dynamic-update-slice_fusion.1
  203.6 0.3 convolution_subtract_fusion
  203.8 11.7 %cholesky.105 = f32[128,128]{1,0:T(8,128)S(1)} custom-call(f32[128,128]{1,0:T(8,128)S(1)} %convolution_subtract_fusion), custom_call_target="Cholesky" | custom-call | tf_op jit(solution)/shard_map/jit(cholesky)/cholesky | solution.py:351
  215.6 0.7 compare_reduce_fusion
  217.7 0.7 select_select_fusion.lower
  218.4 42.3 %shard_map.39 = f32[32,4096]{1,0:T(8,128)} custom-call(f32[384,256]{1,0:T(8,128)} %get-tuple-element.7.mixed, f32[256,256]{1,0:T(8,128)} %select_select_fusion.lower, bf16[384,4096]{1,0:T(8,128)(2,1)} %grads.3), custom_call_target="tpu_custom_call" | custom-call | tf_op jit(solution)/shard_map/pallas_call | solution.py:296
  260.6 1.9 copy.8
  (4 shorter events, 0.1 us)

commit v3 on v2

--- a/solution.py
+++ b/solution.py
@@ -201,6 +201,10 @@
         lanes = slice(way * half, (way + 1) * half)
         mixed[:, lanes] += nt(acts[:, columns], ref[lanes, :])
 
+    def add_gram(pos):
+        block = held.at[pos]
+        gram[...] += nt(block[...], block[...])
+
     ring.barrier(m)
     for piece in range(PIECES):
         for way in WAYS:
@@ -218,6 +222,8 @@
         for way in WAYS:
             pos = ring.at(-s) if way == 0 else ring.at(s)
             add(way, pos, held.at[pos])
+        pl.when(2 * s >= n)(lambda: add_gram(ring.at(s)))
+        pl.when(2 * s > n)(lambda: add_gram(ring.at(-s)))
         return carry
 
     lax.fori_loop(1, n - 1, step, 0)
@@ -228,12 +234,8 @@
         pos = ring.at(1 - n) if way == 0 else ring.at(n - 1)
         add(way, pos, held.at[pos])
 
-    def more(s, carry):
-        block = held.at[ring.at(s)]
-        gram[...] += nt(block[...], block[...])
-        return carry
-
-    lax.fori_loop(1, n, more, 0)
+    add_gram(ring.at(n - 1))
+    add_gram(ring.at(1 - n))
     wid_sum(m, part, got, mine, full, wid_sems)
     out_mixed[...] = full[0:tokens, :]
     out_gram[...] = full[tokens : part.shape[0], :]
@@ -266,8 +268,39 @@
     lax.fori_loop(0, (lower.shape[0] - 1).bit_length(), level, 0)
 
 
+def factor(gram, rest, upper):
+    size = gram.shape[0]
+    block = math.gcd(size, 32)
+    lane = lax.broadcasted_iota(jnp.int32, (block, size), 1)
+    line = lax.broadcasted_iota(jnp.int32, (block, size), 0)
+    one_line = lax.broadcasted_iota(jnp.int32, (block, 1), 0)
+    rest[...] = gram[...]
+
+    def step(k, carry):
+        first = pl.multiple_of(k * block, block)
+        rows = rest[pl.ds(first, block), :]
+        for j in range(block):
+            picked = jnp.where(lane == first + j, rows, 0.0)
+            column = jnp.sum(picked, axis=1, keepdims=True)
+            ratio = jnp.where(one_line > j, column / column[j : j + 1, :], 0.0)
+            rows = rows - ratio * rows[j : j + 1, :]
+        diagonal = jnp.sum(
+            jnp.where(lane == first + line, rows, 0.0), axis=1, keepdims=True
+        )
+        rows = jnp.where(lane >= first + line, rows / jnp.sqrt(diagonal), 0.0)
+        upper[pl.ds(first, block), :] = rows
+        rest[...] -= lax.dot_general(
+            rows, rows, (((0,), (0,)), ((), ())),
+            precision=lax.Precision.HIGHEST, preferred_element_type=F32,
+        )
+        return carry
+
+    lax.fori_loop(0, size // block, step, 0)
+
+
 def coeffs_kernel(
-    n, scale, mixed, lower, grads, out, inverse, terms, send, recv, send_sems, recv_sems
+    n, scale, mixed, gram, grads, out, rest, lower, inverse, terms,
+    send, recv, send_sems, recv_sems,
 ):
     ring = Ring(n)
     rows, width = out.shape
@@ -282,6 +315,8 @@
         out[:, first : first + part] = total
 
     ring.barrier()
+    factor(gram, rest, inverse)
+    lower[...] = inverse[...].T
     invert(lower, inverse)
     proj_t = nt(inverse[...], mixed[...], lax.Precision.HIGHEST).astype(BF16)
     for first in range(0, width, 512 if width % 512 == 0 else width):
@@ -348,15 +383,15 @@
         + [pltpu.VMEM((n, rank, width), BF16)] + sems(n),
         1, acts, rows_t,
     )
-    lower = jnp.linalg.cholesky(gram)
     scale = 1.0 / math.sqrt(tokens * n)
     rows = rank // n
     return call(
         functools.partial(coeffs_kernel, n, scale),
         struct((rows, model), F32),
-        [pltpu.VMEM((rank, rank), F32), pltpu.VMEM((n, rows, model), F32)]
+        [pltpu.VMEM((rank, rank), F32) for _ in range(3)]
+        + [pltpu.VMEM((n, rows, model), F32)]
         + slots(n, rows, model // (2 * PIECES)) + sems(n),
-        2, mixed, lower, out_grads,
+        2, mixed, gram, out_grads,
     )
 
 

time: 263 us -> 248 us (0.943)
  other arithmetic: 35.7 us -> 0 us
  Pallas kernels: 222 us -> 246 us
    another operation x6 -> x0, other arithmetic: 34 us -> none  [ring_shards(): lower = jnp.linalg.cholesky(gram)]
    pallas_call x3, Pallas kernels: 222 us -> 246 us  [call(): pl.pallas_call(kernel, out_shape=outs, in_specs=[vmem] * len(args), out_s...]
where the time goes in v3:
time: 248 us
  Pallas kernels  246 us (99%)
    pallas_call x3, Pallas kernels, call(): pl.pallas_call(kernel, out_shape=outs, in_specs=[vmem] * len(args), out_s...  246 us

profile of v3, /device:TPU:0, one launch (start us, length us, event | category | flops | bytes accessed | tf_op | source)
XLA Modules:
  0.0 247.6 jit_solution(17634185605003897049)
XLA Ops:
  0.0 88.5 %shard_map.37.own = bf16[256,1664]{1,0:T(8,128)(2,1)} custom-call(bf16[384,13312]{1,0:T(8,128)(2,1)} %acts.3, bf16[384,4096]{1,0:T(8,128)(2,1)} %grads.3, bf16[4096,256]{1,0:T(8,128)(2,1)} %test.1), custom_call_target="tpu_custom_call" | custom-call | tf_op jit(solution)/shard_map/pallas_call | solution.py:331
  88.5 88.4 %shard_map.38 = (f32[384,256]{1,0:T(8,128)}, f32[256,256]{1,0:T(8,128)}) custom-call(bf16[384,13312]{1,0:T(8,128)(2,1)} %acts.3, bf16[256,1664]{1,0:T(8,128)(2,1)} %shard_map.37.own), custom_call_target="tpu_custom_call" | custom-call | tf_op jit(solution)/shard_map/pallas_call | solution.py:331
  176.9 68.8 %shard_map.39 = f32[32,4096]{1,0:T(8,128)} custom-call(f32[384,256]{1,0:T(8,128)} %get-tuple-element.7.mixed, f32[256,256]{1,0:T(8,128)} %get-tuple-element.8.gram, bf16[384,4096]{1,0:T(8,128)(2,1)} %grads.3), custom_call_target="tpu_custom_call" | custom-call | tf_op jit(solution)/shard_map/pallas_call | solution.py:331
  245.7 1.9 copy.5

commit v4 on v3

--- a/solution.py
+++ b/solution.py
@@ -13,7 +13,7 @@
 BF16 = jnp.bfloat16
 VMEM_LIMIT = 60 * 1024 * 1024
 WAYS = (0, 1)
-PIECES = 2
+PIECES = 4
 
 
 def nt(a, b, precision=None):

time: 248 us -> 247 us (level)
  no operation moved by 1% of the time
where the time goes in v4:
time: 247 us
  Pallas kernels  245 us (99%)
    pallas_call x3, Pallas kernels, call(): pl.pallas_call(kernel, out_shape=outs, in_specs=[vmem] * len(args), out_s...  245 us

profile of v4, /device:TPU:0, one launch (start us, length us, event | category | flops | bytes accessed | tf_op | source)
XLA Modules:
  0.0 246.6 jit_solution(15595758242534584597)
XLA Ops:
  0.0 89.1 %shard_map.37.own = bf16[256,1664]{1,0:T(8,128)(2,1)} custom-call(bf16[384,13312]{1,0:T(8,128)(2,1)} %acts.3, bf16[384,4096]{1,0:T(8,128)(2,1)} %grads.3, bf16[4096,256]{1,0:T(8,128)(2,1)} %test.1), custom_call_target="tpu_custom_call" | custom-call | tf_op jit(solution)/shard_map/pallas_call | solution.py:331
  89.1 88.9 %shard_map.38 = (f32[384,256]{1,0:T(8,128)}, f32[256,256]{1,0:T(8,128)}) custom-call(bf16[384,13312]{1,0:T(8,128)(2,1)} %acts.3, bf16[256,1664]{1,0:T(8,128)(2,1)} %shard_map.37.own), custom_call_target="tpu_custom_call" | custom-call | tf_op jit(solution)/shard_map/pallas_call | solution.py:331
  178.1 66.7 %shard_map.39 = f32[32,4096]{1,0:T(8,128)} custom-call(f32[384,256]{1,0:T(8,128)} %get-tuple-element.7.mixed, f32[256,256]{1,0:T(8,128)} %get-tuple-element.8.gram, bf16[384,4096]{1,0:T(8,128)(2,1)} %grads.3), custom_call_target="tpu_custom_call" | custom-call | tf_op jit(solution)/shard_map/pallas_call | solution.py:331
  244.7 1.9 copy.5
